TPU v7x, 32 devices: a whole 2x2x4 slice. The times are simulated.
32 devices in a mesh: scen: 8 (over z, x), row: 2 (over y), col: 2 (over core).
Axes of the slice: x: 2, y: 2, z: 4, core: 2. Of those that a mesh axis runs over, the one named last changes fastest.
Arguments:
- coupling: bfloat16 [24, 512, 3072], P('scen', None, ('row', 'col')), may hold values from -0.078125 to 0.078125
- factor_inv: bfloat16 [24, 512, 512], P('scen'), as said below
- block_mask: int32 [24, 4, 24], P('scen', None, ('row', 'col')), may hold values 0 or 1
Outputs:
- schur: float32 [2, 1536, 2, 2, 768], P('row', 'scen', None, 'col')
Inputs may be any that keep to these rules, and one draw needn't show every extreme that they name: factor_inv is lower triangular with a positive diagonal.
All inputs are finite; a program needn't handle non-finite values. No bound on the sum of `block_mask` on one device may be relied on, other than what follows from the above.
Results may differ from a plain program's by a relative error of at most 0.00064.
Values may be sent and summed in bfloat16 or wider, within the bound.
A program may use at most 64 MiB of HBM per device.

v0:
```python
import functools

import jax
import jax.numpy as jnp
from jax import lax
from jax.experimental import pallas as pl
from jax.experimental.pallas import tpu as pltpu
from jax.sharding import PartitionSpec as P

BLK = 128
PIECE = 256
HALF = PIECE // 2
HEAD = 16
LINK = jnp.int16
FINE = 64.0
TOP = 14.9
STARTS = (4, 7, 9, 10)
MESH = pl.DeviceIdType.MESH
NT = (((1,), (1,)), ((), ()))


def encode(value):
    most = jnp.maximum(jnp.max(jnp.abs(value), axis=0, keepdims=True), 1e-30)
    power = jnp.ceil(jnp.log2(most) * FINE)
    scaled = jnp.round(value * jnp.exp2(TOP - power / FINE))
    head = jnp.broadcast_to(power, (HEAD, value.shape[1]))
    return head.astype(jnp.int32).astype(LINK), scaled.astype(jnp.int32).astype(LINK)


def decode(head, scaled):
    power = head.astype(jnp.int32).astype(jnp.float32)[0:1, :]
    return scaled.astype(jnp.int32).astype(jnp.float32) * jnp.exp2(power / FINE - TOP)


def kernel(n, n_row, coupling, factor, mask, out, left, right,
           col_send, col_recv, row_send, row_recv, ring_send, ring_recv, *buffers):
    groups, order, width = coupling.shape
    share = out.shape[0]
    phases = phases_of(n_row, width)
    partial, held, sent = [buffers[i * len(phases):(i + 1) * len(phases)] for i in range(3)]
    late = sorted({phase[1:3] for phase in phases if phase[0]})
    scen, row, col = lax.axis_index("scen"), lax.axis_index("row"), lax.axis_index("col")

    half = n // 2
    side, depth = lax.rem(scen, 2), scen // 2
    place = jnp.where(side == 0, depth, n - 1 - depth)

    def at(position):
        position = lax.rem(position + 2 * n, n)
        return jnp.where(position < half, 2 * position, 2 * (n - 1 - position) + 1)

    around = (at(place + 1), at(place - 1))
    partners = [lax.rem(row + n_row - d, n_row) for d in range(1, n_row)]
    barrier = pltpu.get_barrier_semaphore()
    for target in around:
        pl.semaphore_signal(barrier, inc=1, device_id=(target, row, col), device_id_type=MESH)
    for target in partners:
        pl.semaphore_signal(barrier, inc=1, device_id=(scen, target, col), device_id_type=MESH)
    pl.semaphore_signal(barrier, inc=1, device_id=(scen, row, 1 - col), device_id_type=MESH)

    mine = pl.ds(pl.multiple_of(col * width, width), width)
    col_copies, row_copies = [], {}

    def row_send_piece(g, k):
        base, count = late[k]
        for d in range(1, n_row):
            copy = pltpu.make_async_remote_copy(
                src_ref=left.at[g, pl.ds(pl.multiple_of(col * width + base, HALF), count)],
                dst_ref=right.at[d - 1, g, pl.ds(base, count)],
                send_sem=row_send.at[d - 1, k, g], recv_sem=row_recv.at[d - 1, k, g],
                device_id=(scen, partners[d - 1], col), device_id_type=MESH)
            copy.start()
            row_copies[d, base, g] = copy

    for g in range(groups):
        rows = []
        for i in range(order // BLK):
            rows.append(jnp.concatenate([
                coupling[g, i * BLK:(i + 1) * BLK, j * BLK:(j + 1) * BLK]
                * mask[g, i, j].astype(jnp.float32).astype(jnp.bfloat16)
                for j in range(width // BLK)], axis=1))
        masked = jnp.concatenate(rows, axis=0)
        solved = jnp.dot(factor[g], masked, preferred_element_type=jnp.float32)
        left[g, mine, :] = solved.T.astype(jnp.bfloat16)
        if g == 0:
            pl.semaphore_wait(barrier, 2 + n_row)
        copy = pltpu.make_async_remote_copy(
            src_ref=left.at[g, mine], dst_ref=left.at[g, mine],
            send_sem=col_send.at[g], recv_sem=col_recv.at[g],
            device_id=(scen, row, 1 - col), device_id_type=MESH)
        copy.start()
        col_copies.append(copy)
        row_send_piece(g, 0)
    for k in range(1, len(late)):
        for g in range(groups):
            row_send_piece(g, k)

    ring_copies = {}

    def multiply(phase, b):
        d, base, count, _ = phases[phase]

        def block(g):
            if d:
                return right[d - 1, g, base:base + count, :]
            return left[g, pl.ds(pl.multiple_of(col * width + base, HALF), count), :]

        rows = pl.ds(pl.multiple_of(b * width, width), width)
        total = lax.dot_general(left[0, rows, :], block(0), NT, preferred_element_type=jnp.float32)
        for g in range(1, groups):
            total += lax.dot_general(left[g, rows, :], block(g), NT, preferred_element_type=jnp.float32)
        partial[phase][pl.ds(b * half, half)] = total.reshape(half, share, count)

    def hop(phase, way, step):
        d, base, count, by_rows = phases[phase]
        if by_rows:
            rows, lanes = slice(way * share // 2, (way + 1) * share // 2), slice(0, count)
        else:
            rows, lanes = slice(0, share), slice(way * count // 2, (way + 1) * count // 2)
        chunk = at(place - 1 - step) if way == 0 else at(place + 1 + step)
        value = partial[phase][chunk, rows, lanes]
        if step:
            ring_copies[phase, way, step - 1].wait_recv()
            came = held[phase]
            value += decode(came[way, step - 1, 0:HEAD, :], came[way, step - 1, HEAD:, :])
        if step == n - 1:
            start = lax.rem(row + d, n_row) * width + base + lanes.start
            out[rows, pl.ds(pl.multiple_of(start, HALF), lanes.stop - lanes.start)] = value
            return
        head, scaled = encode(value)
        sent[phase][way, step, 0:HEAD, :] = head
        sent[phase][way, step, HEAD:, :] = scaled
        copy = pltpu.make_async_remote_copy(
            src_ref=sent[phase].at[way, step], dst_ref=held[phase].at[way, step],
            send_sem=ring_send.at[phase, way, step], recv_sem=ring_recv.at[phase, way, step],
            device_id=(around[way], row, col), device_id_type=MESH)
        copy.start()
        ring_copies[phase, way, step] = copy

    early = [phase for phase in range(len(phases)) if phases[phase][0] == 0]
    for phase in early:
        multiply(phase, col)
    for copy in col_copies:
        copy.wait_recv()
    starts = [0 if phase in early else STARTS[min(late.index(phases[phase][1:3]), len(STARTS) - 1)]
              for phase in range(len(phases))]
    for tick in range(max(starts) + n):
        for phase, start in enumerate(starts):
            step = tick - start
            if step == 0 and phase in early:
                multiply(phase, 1 - col)
            elif step == 0:
                d, base = phases[phase][:2]
                for g in range(groups):
                    row_copies[d, base, g].wait_recv()

                @pl.loop(0, 2)
                def _(b):
                    multiply(phase, b)
            if 0 <= step < n:
                hop(phase, 0, step)
                hop(phase, 1, step)
    for copy in col_copies + list(row_copies.values()) + list(ring_copies.values()):
        copy.wait_send()


def phases_of(n_row, width):
    early = [(0, base, PIECE, False) for base in range(0, width, PIECE)]
    late = [(base, PIECE, False) for base in range(0, width - PIECE, PIECE)]
    late += [(base, HALF, True) for base in (width - PIECE, width - HALF)]
    return early + [(d, *piece) for piece in late for d in range(1, n_row)]


def fused(n, n_row, coupling, factor_inv, block_mask):
    groups, order, width = coupling.shape
    rows = 2 * width
    share = rows // n
    phases = phases_of(n_row, width)
    late = len(phases) - width // PIECE
    shapes = [(2, n - 1, HEAD + (share // 2 if by_rows else share), HALF) for _, _, _, by_rows in phases]
    partials = [pltpu.VMEM((n, share, count), jnp.float32) for _, _, count, _ in phases]
    messages = [pltpu.VMEM(shape, LINK) for shape in shapes]
    vmem = pl.BlockSpec(memory_space=pltpu.VMEM)
    tile = pl.pallas_call(
        functools.partial(kernel, n, n_row),
        out_shape=jax.ShapeDtypeStruct((share, n_row * width), jnp.float32),
        in_specs=[vmem, vmem, pl.BlockSpec(memory_space=pltpu.SMEM)],
        out_specs=vmem,
        scratch_shapes=[
            pltpu.VMEM((groups, rows, order), jnp.bfloat16),
            pltpu.VMEM((n_row - 1, groups, width, order), jnp.bfloat16),
            pltpu.SemaphoreType.DMA((groups,)),
            pltpu.SemaphoreType.DMA((groups,)),
            pltpu.SemaphoreType.DMA((n_row - 1, late, groups)),
            pltpu.SemaphoreType.DMA((n_row - 1, late, groups)),
            pltpu.SemaphoreType.DMA((len(phases), 2, n - 1)),
            pltpu.SemaphoreType.DMA((len(phases), 2, n - 1)),
            *partials, *messages, *messages,
        ],
        compiler_params=pltpu.CompilerParams(
            collective_id=0, has_side_effects=True, vmem_limit_bytes=60 * 1024 * 1024),
    )(coupling, factor_inv, block_mask)
    return tile.reshape(1, share, n_row, 1, width)


def plain(coupling, factor_inv, block_mask):
    groups, order, width = coupling.shape
    spread = jnp.broadcast_to(
        block_mask[:, :, None, :, None], (groups, order // BLK, BLK, width // BLK, BLK)
    )
    masked = coupling * spread.reshape(groups, order, width).astype(jnp.bfloat16)
    solved = jnp.einsum(
        "snk,skw->snw", factor_inv, masked, preferred_element_type=jnp.float32
    ).astype(jnp.bfloat16)
    left = lax.all_gather(solved, "col", axis=2, tiled=True)
    share = left.shape[2] // lax.axis_size("scen")
    tile = lax.dot_general(
        left,
        lax.all_gather(solved, "row", axis=2, tiled=True),
        (((0, 1), (0, 1)), ((), ())),
        preferred_element_type=jnp.float32,
    )
    summed = lax.psum_scatter(tile, "scen", scatter_dimension=0, tiled=True)
    return summed.reshape(1, share, summed.shape[1] // width, 1, width)


def solution(mesh):
    n, n_row = mesh.shape["scen"], mesh.shape["row"]

    def shards(coupling, factor_inv, block_mask):
        width = coupling.shape[2]
        share = 2 * width // n
        if share % 32 == 0 and width % PIECE == 0 and n % 2 == 0 and n > 2 and n_row > 1:
            return fused(n, n_row, coupling, factor_inv, block_mask)
        return plain(coupling, factor_inv, block_mask)

    in_specs = (
        P("scen", None, ("row", "col")),
        P("scen", None, None),
        P("scen", None, ("row", "col")),
    )
    out_specs = P("row", "scen", None, "col", None)
    return jax.shard_map(shards, mesh=mesh, in_specs=in_specs, out_specs=out_specs, check_vma=False)
```

profile of v0, /device:TPU:0, one launch (start us, length us, event | category | flops | bytes accessed | tf_op | source)
XLA Modules:
  0.0 88.5 jit_solution(14246511203167414448)
XLA Ops:
  0.0 84.9 %shard_map.37 = f32[192,1536]{1,0:T(8,128)} custom-call(bf16[3,512,768]{2,1,0:T(8,128)(2,1)} %coupling.1, bf16[3,512,512]{2,1,0:T(8,128)(2,1)} %factor.1, s32[3,4,6]{2,1,0:T(4,128)} %mask.1), custom_call_target="tpu_custom_call" | custom-call | tf_op jit(solution)/shard_map/pallas_call | solution.py:184
  84.9 3.6 %reshape.4 = f32[1,192,2,1,768]{4,3,2,1,0:T(1,128)} reshape(f32[192,1536]{1,0:T(8,128)} %shard_map.37) | data formatting | bytes 2359296 | tf_op jit(solution)/shard_map/reshape | solution.py:203
where the time goes:
time: 88.6 us; the launch traced here: 88.5 us
  Pallas kernels  84.9 us (96%)
  local copies, waits for them, and re-layouts  3.55 us (4%)
    pallas_call x1, Pallas kernels, fused(): pl.pallas_call(functools.partial(kernel, n, n_row), out_shape=jax.ShapeDt...  84.9 us
    reshape x1, local copies, waits for them, and re-layouts, fused(): return tile.reshape(1, share, n_row, 1, width)  3.55 us

commit v1 on v0

v1 whole, which is shorter than its diff:
```python
import functools

import jax
import jax.numpy as jnp
from jax import lax
from jax.experimental import pallas as pl
from jax.experimental.pallas import tpu as pltpu
from jax.sharding import PartitionSpec as P

BLK = 128
LANES = 128
HEAD = 16
LINK = jnp.int16
FINE = 64.0
TOP = 14.9
PIECE = 256
DEPTH = 4
MESH = pl.DeviceIdType.MESH
NT = (((1,), (1,)), ((), ()))
ORDER = (2, 1, 3, 0)


def encode(value):
    most = jnp.maximum(jnp.max(jnp.abs(value), axis=0, keepdims=True), 1e-30)
    power = jnp.ceil(jnp.log2(most) * FINE)
    scaled = jnp.round(value * jnp.exp2(TOP - power / FINE))
    head = jnp.broadcast_to(power, (HEAD, value.shape[1]))
    return head.astype(jnp.int32).astype(LINK), scaled.astype(jnp.int32).astype(LINK)


def decode(head, scaled):
    power = head.astype(jnp.int32).astype(jnp.float32)[0:1, :]
    return scaled.astype(jnp.int32).astype(jnp.float32) * jnp.exp2(power / FINE - TOP)


def pieces_of(width):
    early = [(0, base, PIECE) for base in range(0, width, PIECE)]
    late = [(1, base, PIECE) for base in range(0, width - PIECE, PIECE)]
    late += [(1, width - PIECE, PIECE // 2), (1, width - PIECE // 2, PIECE // 2)]
    return early, late


def kernel(coupling, factor, mask, out, c_in, f_in, own, left, right,
           in_sem, col_send, col_recv, row_send, row_recv,
           x_send, x_recv, z_send, z_recv, away, *buffers):
    groups, order, width = coupling.shape
    share = 2 * width // (2 * DEPTH)
    early, late = pieces_of(width)
    pieces = early + late
    count = len(pieces)
    keep, x_out, x_in, z_out, z_in = [buffers[i * count:(i + 1) * count] for i in range(5)]
    scen, row, col = lax.axis_index("scen"), lax.axis_index("row"), lax.axis_index("col")
    z, x = scen // 2, lax.rem(scen, 2)
    across = (2 * z + 1 - x, row, col)
    opposite = (scen, 1 - row, col)
    sibling = (scen, row, 1 - col)

    def level(d):
        return lax.rem(z + d, DEPTH)

    loads = []
    for g in range(groups):
        for src, dst, k in ((coupling, c_in, 0), (factor, f_in, 1)):
            load = pltpu.make_async_copy(src.at[g], dst.at[g], in_sem.at[g, k])
            load.start()
            loads.append(load)

    barrier = pltpu.get_barrier_semaphore()
    peers = [across, opposite, sibling] + [(2 * level(d) + x, row, col) for d in range(1, DEPTH)]
    for peer in peers:
        pl.semaphore_signal(barrier, inc=1, device_id=peer, device_id_type=MESH)

    copies = []

    def send(src, dst, send_sem, recv_sem, device):
        copy = pltpu.make_async_remote_copy(
            src_ref=src, dst_ref=dst, send_sem=send_sem, recv_sem=recv_sem,
            device_id=device, device_id_type=MESH)
        copy.start()
        copies.append(copy)
        return copy

    col_copies, row_copies = [], {}

    def send_row(k, g):
        _, base, w = late[k]
        row_copies[k, g] = send(
            own.at[g, pl.ds(base, w)], right.at[g, pl.ds(base, w)],
            row_send.at[k, g], row_recv.at[k, g], opposite)

    half = width // 2
    for g in range(groups):
        loads[2 * g].wait()
        loads[2 * g + 1].wait()
        rows = []
        for i in range(order // BLK):
            rows.append(jnp.concatenate([
                c_in[g, i * BLK:(i + 1) * BLK, j * BLK:(j + 1) * BLK]
                * mask[g, i, j].astype(jnp.float32).astype(jnp.bfloat16)
                for j in range(width // BLK)], axis=1))
        masked = jnp.concatenate(rows, axis=0)
        solved = jnp.dot(f_in[g], masked, preferred_element_type=jnp.float32)
        turned = solved.T.astype(jnp.bfloat16)
        own[g] = turned
        for a in range(2):
            for b in range(2):
                at = pl.multiple_of(col * half + a * share, share)
                left[g, b, pl.ds(at, share), :] = turned[(2 * a + b) * share:(2 * a + b + 1) * share]
        if g == 0:
            pl.semaphore_wait(barrier, len(peers))
        send_row(0, g)
        for b in range(2):
            mine = left.at[g, b, pl.ds(pl.multiple_of(col * half, half), half)]
            col_copies.append(send(mine, mine, col_send.at[g, b], col_recv.at[g, b], sibling))
    for k in range(1, len(late)):
        for g in range(groups):
            send_row(k, g)

    def product(b, p):
        kind, base, w = pieces[p]
        source = right if kind else own
        total = None
        for g in range(groups):
            term = lax.dot_general(
                left[g, b], source[g, base:base + w, :], NT, preferred_element_type=jnp.float32)
            total = term if total is None else total + term
        return total

    def slab(d):
        return pl.ds(pl.multiple_of(level(d) * share, share), share)

    def pack(ref, value):
        head, scaled = encode(value)
        ref[0:HEAD, :] = head
        ref[HEAD:, :] = scaled

    def unpack(ref):
        return decode(ref[0:HEAD, :], ref[HEAD:, :])

    x_copies, z_copies = {}, {}

    def multiply(p):
        kind, base, w = pieces[p]
        if kind:
            for g in range(groups):
                row_copies[late.index(pieces[p]), g].wait_recv()
        away[:, 0:w] = product(1 - x, p)
        for d in ORDER:
            pack(x_out[p].at[d], away[slab(d), 0:w])
            x_copies[p, d] = send(x_out[p].at[d], x_in[p].at[d], x_send.at[p, d], x_recv.at[p, d], across)
        keep[p][...] = product(x, p)

    def pass_on(p):
        for d in ORDER:
            x_copies[p, d].wait_recv()
            value = keep[p][slab(d), :] + unpack(x_in[p].at[d])
            if d == 0:
                keep[p][slab(0), :] = value
            else:
                pack(z_out[p].at[d - 1], value)
                z_copies[p, d] = send(
                    z_out[p].at[d - 1], z_in[p].at[d - 1], z_send.at[p, d - 1], z_recv.at[p, d - 1],
                    (2 * level(d) + x, row, col))

    def finish(p):
        kind, base, w = pieces[p]
        value = keep[p][slab(0), :]
        for d in range(1, DEPTH):
            z_copies[p, d].wait_recv()
            value += unpack(z_in[p].at[d - 1])
        lines = width // LANES
        place = (1 - row if kind else row) * lines + base // LANES
        for c in range(w // LANES):
            out[pl.ds(place + c, share, stride=2 * lines), :] = value[:, c * LANES:(c + 1) * LANES]

    for copy in col_copies:
        copy.wait_recv()
    plan = [(multiply, 0), (multiply, 1), (multiply, 2), (pass_on, 0), (pass_on, 1), (multiply, 3),
            (pass_on, 2), (finish, 0), (finish, 1), (multiply, 4), (pass_on, 3), (finish, 2),
            (multiply, 5), (pass_on, 4), (finish, 3), (multiply, 6), (pass_on, 5), (pass_on, 6),
            (finish, 4), (finish, 5), (finish, 6)]
    for task, p in plan:
        task(p)
    for copy in copies:
        copy.wait_send()


def fused(coupling, factor_inv, block_mask):
    groups, order, width = coupling.shape
    share = 2 * width // (2 * DEPTH)
    early, late = pieces_of(width)
    pieces = early + late
    count = len(pieces)
    hbm = pl.BlockSpec(memory_space=pl.ANY)
    message = HEAD + share
    tile = pl.pallas_call(
        kernel,
        out_shape=jax.ShapeDtypeStruct((share * 2 * width // LANES, LANES), jnp.float32),
        in_specs=[hbm, hbm, pl.BlockSpec(memory_space=pltpu.SMEM)],
        out_specs=pl.BlockSpec(memory_space=pltpu.VMEM),
        scratch_shapes=[
            pltpu.VMEM((groups, order, width), jnp.bfloat16),
            pltpu.VMEM((groups, order, order), jnp.bfloat16),
            pltpu.VMEM((groups, width, order), jnp.bfloat16),
            pltpu.VMEM((groups, 2, width, order), jnp.bfloat16),
            pltpu.VMEM((groups, width, order), jnp.bfloat16),
            pltpu.SemaphoreType.DMA((groups, 2)),
            pltpu.SemaphoreType.DMA((groups, 2)),
            pltpu.SemaphoreType.DMA((groups, 2)),
            pltpu.SemaphoreType.DMA((len(late), groups)),
            pltpu.SemaphoreType.DMA((len(late), groups)),
            pltpu.SemaphoreType.DMA((count, DEPTH)),
            pltpu.SemaphoreType.DMA((count, DEPTH)),
            pltpu.SemaphoreType.DMA((count, DEPTH - 1)),
            pltpu.SemaphoreType.DMA((count, DEPTH - 1)),
            pltpu.VMEM((width, PIECE), jnp.float32),
            *[pltpu.VMEM((width, w), jnp.float32) for _, _, w in pieces],
            *[pltpu.VMEM((DEPTH, message, w), LINK) for _, _, w in pieces],
            *[pltpu.VMEM((DEPTH, message, w), LINK) for _, _, w in pieces],
            *[pltpu.VMEM((DEPTH - 1, message, w), LINK) for _, _, w in pieces],
            *[pltpu.VMEM((DEPTH - 1, message, w), LINK) for _, _, w in pieces],
        ],
        compiler_params=pltpu.CompilerParams(
            collective_id=0, has_side_effects=True, vmem_limit_bytes=60 * 1024 * 1024),
    )(coupling, factor_inv, block_mask)
    return tile.reshape(1, share, 2, 1, width)


def plain(coupling, factor_inv, block_mask):
    groups, order, width = coupling.shape
    spread = jnp.broadcast_to(
        block_mask[:, :, None, :, None], (groups, order // BLK, BLK, width // BLK, BLK)
    )
    masked = coupling * spread.reshape(groups, order, width).astype(jnp.bfloat16)
    solved = jnp.einsum(
        "snk,skw->snw", factor_inv, masked, preferred_element_type=jnp.float32
    ).astype(jnp.bfloat16)
    left = lax.all_gather(solved, "col", axis=2, tiled=True)
    share = left.shape[2] // lax.axis_size("scen")
    tile = lax.dot_general(
        left,
        lax.all_gather(solved, "row", axis=2, tiled=True),
        (((0, 1), (0, 1)), ((), ())),
        preferred_element_type=jnp.float32,
    )
    summed = lax.psum_scatter(tile, "scen", scatter_dimension=0, tiled=True)
    return summed.reshape(1, share, summed.shape[1] // width, 1, width)


def solution(mesh):
    n, n_row = mesh.shape["scen"], mesh.shape["row"]

    def shards(coupling, factor_inv, block_mask):
        groups, order, width = coupling.shape
        if n == 2 * DEPTH and n_row == 2 and width == 3 * PIECE and order % BLK == 0 and groups <= 4:
            return fused(coupling, factor_inv, block_mask)
        return plain(coupling, factor_inv, block_mask)

    in_specs = (
        P("scen", None, ("row", "col")),
        P("scen", None, None),
        P("scen", None, ("row", "col")),
    )
    out_specs = P("row", "scen", None, "col", None)
    return jax.shard_map(shards, mesh=mesh, in_specs=in_specs, out_specs=out_specs, check_vma=False)
```

time: 88.6 us -> 79.1 us (0.89)
  Pallas kernels: 84.9 us -> 75.8 us
    pallas_call x1, Pallas kernels: 84.9 us -> 75.8 us  [fused(): pl.pallas_call(kernel, out_shape=jax.ShapeDtypeStruct((share * 2 * width...]
    reshape x1 -> x0, local copies, waits for them, and re-layouts: 3.55 us -> none  [fused(): return tile.reshape(1, share, n_row, 1, width)]
    unnamed x0 -> x1, local copies, waits for them, and re-layouts: none -> 3.09 us
where the time goes in v1:
time: 79.1 us; the launch traced here: 78.9 us
  Pallas kernels  75.8 us (96%)
  local copies, waits for them, and re-layouts  3.09 us (4%)
    pallas_call x1, Pallas kernels, fused(): pl.pallas_call(kernel, out_shape=jax.ShapeDtypeStruct((share * 2 * width...  75.8 us
    unnamed x1, local copies, waits for them, and re-layouts  3.09 us

profile of v1, /device:TPU:0, one launch (start us, length us, event | category | flops | bytes accessed | tf_op | source)
XLA Modules:
  0.0 78.9 jit_solution(10937867055938291504)
XLA Ops:
  0.0 75.8 %shard_map.37 = f32[2304,128]{1,0:T(8,128)} custom-call(bf16[3,512,768]{2,1,0:T(8,128)(2,1)} %coupling.1, bf16[3,512,512]{2,1,0:T(8,128)(2,1)} %factor.1, s32[3,4,6]{2,1,0:T(4,128)} %mask.1), custom_call_target="tpu_custom_call" | custom-call | tf_op jit(solution)/shard_map/pallas_call | solution.py:196
  75.8 3.1 %copy.6 = f32[1,192,2,1,768]{4,3,2,1,0:T(1,128)} copy(f32[1,192,2,1,768]{4,3,2,1,0:T(1,128)} %bitcast.1) | data formatting | bytes 2359296

commit v2 on v1

v2 whole, which is shorter than its diff:
```python
import functools

import jax
import jax.numpy as jnp
from jax import lax
from jax.experimental import pallas as pl
from jax.experimental.pallas import tpu as pltpu
from jax.sharding import PartitionSpec as P

BLK = 128
LANES = 128
HEAD = 16
LINK = jnp.int16
FINE = 64.0
TOP = 14.9
DEPTH = 4
MESH = pl.DeviceIdType.MESH
NT = (((1,), (1,)), ((), ()))
PIECES = ((0, 3), (0, 2), (1, DEPTH), (1, DEPTH))
SWAPS = ((0, 1), (0, 2), (1, 1), (2, 0), (3, 0))
GROUPS = ((0, (0,)), (0, (1, 2)), (1, (1,)), (2, (3, 2)), (2, (1, 0)), (3, (3,)), (3, (2,)), (3, (1,)), (3, (0,)), (1, (0,)))


def power_of(values):
    most = jnp.max(jnp.abs(values[0]), axis=0, keepdims=True)
    for value in values[1:]:
        most = jnp.maximum(most, jnp.max(jnp.abs(value), axis=0, keepdims=True))
    return jnp.ceil(jnp.log2(jnp.maximum(most, 1e-30)) * FINE)


def pack(ref, values):
    power = power_of(values)
    scale = jnp.exp2(TOP - power / FINE)
    ref[0:HEAD, :] = jnp.broadcast_to(power, (HEAD, power.shape[1])).astype(jnp.int32).astype(LINK)
    start = HEAD
    for value in values:
        count = value.shape[0]
        ref[start:start + count, :] = jnp.round(value * scale).astype(jnp.int32).astype(LINK)
        start += count


def unpack(ref, start, count):
    power = ref[0:HEAD, :].astype(jnp.int32).astype(jnp.float32)[0:1, :]
    scaled = ref[HEAD + start:HEAD + start + count, :].astype(jnp.int32).astype(jnp.float32)
    return scaled * jnp.exp2(power / FINE - TOP)


def keys_of():
    keys = [(p, e) for p, (_, size) in enumerate(PIECES) for e in range(size)]
    return {key: i for i, key in enumerate(keys)}


def when(condition, action):
    if condition is True:
        action()
    elif condition is not False:
        pl.when(condition)(action)


def kernel(coupling, factor, mask, out, c_in, f_in, own, left, right, keep, away, joined,
           z_out, near_in, far_in, swap_out, swap_in,
           in_sem, col_send, col_recv, row_send, row_recv, x_send, x_recv,
           near_recv, far_recv, z_send, swap_send, swap_recv, *buffers):
    groups, order, width = coupling.shape
    depth = groups * order
    part = depth // 2
    share = width // DEPTH
    block = 2 * share
    lines = width // LANES
    wide = block // LANES
    x_out, x_in = buffers[:len(GROUPS)], buffers[len(GROUPS):]
    scen, row, col = lax.axis_index("scen"), lax.axis_index("row"), lax.axis_index("col")
    z, x = scen // 2, lax.rem(scen, 2)
    near = z + 1 - 2 * lax.rem(z, 2)
    far = lax.rem(z + 2, DEPTH)
    last = DEPTH - 1 - z
    apart = (z, near, far, last)
    across = (2 * z + 1 - x, row, col)
    opposite = (scen, 1 - row, col)
    sibling = (scen, row, 1 - col)
    index = keys_of()

    turn = [jnp.where(row == 0, groups - 1 - g, g) for g in range(groups)]
    loads = []
    for g in range(groups):
        pair = []
        for src, dst, k in ((coupling, c_in, 0), (factor, f_in, 1)):
            load = pltpu.make_async_copy(src.at[turn[g]], dst.at[g], in_sem.at[g, k])
            load.start()
            pair.append(load)
        loads.append(pair)

    barrier = pltpu.get_barrier_semaphore()
    peers = [across, opposite, sibling] + [(2 * level + x, row, col) for level in apart[1:]]
    for peer in peers:
        pl.semaphore_signal(barrier, inc=1, device_id=peer, device_id_type=MESH)

    pending = []

    def remote(src, dst, send_sem, recv_sem, device, condition=True):
        copy = pltpu.make_async_remote_copy(
            src_ref=src, dst_ref=dst, send_sem=send_sem, recv_sem=recv_sem,
            device_id=device, device_id_type=MESH)
        pending.append((copy, condition))
        return copy

    col_copies, row_copies = [], {}

    def send_row(half, chunk):
        if chunk == 0:
            size, start, to = order, jnp.where(row == 0, depth - order, 0), jnp.where(row == 0, part - order, 0)
        else:
            size, start, to = part - order, jnp.where(row == 0, part, order), jnp.where(row == 0, 0, order)
        rows = pl.ds(half * block, block)
        copy = remote(
            own.at[rows, pl.ds(pl.multiple_of(start, 256), size)],
            right.at[rows, pl.ds(pl.multiple_of(to, 256), size)],
            row_send.at[half, chunk], row_recv.at[half, chunk], opposite)
        copy.start()
        back = pltpu.make_async_copy(
            right.at[rows, pl.ds(pl.multiple_of(part - size - to, 256), size)],
            right.at[rows, pl.ds(pl.multiple_of(part - size - to, 256), size)], row_recv.at[half, chunk])
        row_copies[half, chunk] = back

    for g in range(groups):
        for load in loads[g]:
            load.wait()
        rows = []
        for i in range(order // BLK):
            rows.append(jnp.concatenate([
                c_in[g, i * BLK:(i + 1) * BLK, j * BLK:(j + 1) * BLK]
                * mask[turn[g], i, j].astype(jnp.float32).astype(jnp.bfloat16)
                for j in range(width // BLK)], axis=1))
        masked = jnp.concatenate(rows, axis=0)
        solved = jnp.dot(f_in[g], masked, preferred_element_type=jnp.float32)
        turned = solved.T.astype(jnp.bfloat16)
        lanes = pl.ds(pl.multiple_of(turn[g] * order, order), order)
        own[:, lanes] = turned
        for a in range(2):
            for b in range(2):
                at = pl.multiple_of(col * block + a * share, share)
                left[b, pl.ds(at, share), lanes] = turned[(2 * a + b) * share:(2 * a + b + 1) * share]
        if g == 0:
            pl.semaphore_wait(barrier, len(peers))
            send_row(0, 0)
        elif g == 1:
            send_row(0, 1)
            send_row(1, 0)
            send_row(1, 1)
        mine = left.at[:, pl.ds(pl.multiple_of(col * block, block), block), lanes]
        copy = remote(mine, mine, col_send.at[g], col_recv.at[g], sibling)
        copy.start()
        col_copies.append(copy)

    def column(p):
        return (3 * col, 1 + col, 2 * col, 2 * col + 1)[p]

    def level(p, e):
        return apart[e] if PIECES[p][0] else lax.rem(column(p) + e, DEPTH)

    def product(b, p, e):
        rows = pl.ds(pl.multiple_of(level(p, e) * share, share), share)
        if PIECES[p][0]:
            lhs = left[b, rows, pl.ds(pl.multiple_of(row * part, 256), part)]
            rhs = right[(p - 2) * block:(p - 1) * block, :]
        else:
            lhs = left[b, rows, :]
            rhs = own[pl.ds(pl.multiple_of((col if p == 0 else 1 - col) * block, block), block), :]
        return lax.dot_general(lhs, rhs, NT, preferred_element_type=jnp.float32)

    place_of = {(p, e): (k, i) for k, (p, es) in enumerate(GROUPS) for i, e in enumerate(es)}
    x_copies, near_copies, far_copies, swaps = {}, {}, {}, {}

    def multiply(k):
        p, es = GROUPS[k]
        for i, e in enumerate(es):
            away[i] = product(1 - x, p, e)
        pack(x_out[k], [away[i] for i in range(len(es))])
        copy = remote(x_out[k], x_in[k], x_send.at[k], x_recv.at[k], across)
        copy.start()
        x_copies[k] = copy

    def retain(k):
        p, es = GROUPS[k]
        for e in es:
            keep[index[p, e]] = product(x, p, e)

    def roles(p, e):
        if PIECES[p][0]:
            return e == 0, e % 2 == 1, e == 2
        at = level(p, e)
        return z == at, lax.rem(z + at, 2) == 1, far == at

    def direct(p):
        return p == 3

    def take(p, e):
        k, i = place_of[p, e]
        if i == 0:
            x_copies[k].wait_recv()
        me = index[p, e]
        final, differ, relay = roles(p, e)
        keep[me] = keep[me] + unpack(x_in[k], i * share, share)
        if direct(p):
            if e:
                pack(z_out.at[me], [keep[me]])
                copy = remote(z_out.at[me], near_in.at[me], z_send.at[me], near_recv.at[me],
                              (2 * level(p, e) + x, row, col))
                copy.start()
                near_copies[p, e] = copy
            return
        to = index[p, e - 1] if PIECES[p][0] and e % 2 else me
        copy = remote(z_out.at[me], near_in.at[to], z_send.at[me], near_recv.at[to],
                      (2 * near + x, row, col), differ)
        near_copies[p, e] = copy if to == me else pltpu.make_async_copy(
            near_in.at[to], near_in.at[to], near_recv.at[to])
        if PIECES[p][0] and e % 2 == 0:
            pending.pop()

        def go():
            pack(z_out.at[me], [keep[me]])
            copy.start()

        when(differ, go)

    def relay(p, e):
        if direct(p):
            return
        me = index[p, e]
        final, differ, relayed = roles(p, e)
        if differ is True:
            return
        same = (not differ) if isinstance(differ, bool) else jnp.logical_not(differ)
        arrived = pltpu.make_async_copy(near_in.at[me], near_in.at[me], near_recv.at[me])
        to = index[p, 0] if PIECES[p][0] else me
        copy = None
        if relayed is not False:
            copy = remote(z_out.at[me], far_in.at[to], z_send.at[me], far_recv.at[to],
                          (2 * far + x, row, col), relayed)

        def add():
            arrived.wait()
            keep[me] = keep[me] + unpack(near_in.at[me], 0, share)

        when(same, add)
        if copy is not None:
            def go():
                pack(z_out.at[me], [keep[me]])
                copy.start()

            when(relayed, go)

    def show(place, value):
        for c in range(wide):
            out[pl.ds(place + c, share, stride=2 * lines), :] = value[:, c * LANES:(c + 1) * LANES]

    def finish(p, e):
        kind = PIECES[p][0]
        me = index[p, e]
        final = roles(p, e)[0]
        at = level(p, e)
        copies = []
        if (p, e) in SWAPS:
            s = SWAPS.index((p, e))
            side = 1 - row if kind else row
            for b in range(2):
                copies.append(remote(
                    swap_out.at[s, b], swap_in.at[kind, lax.rem(at, 2), x],
                    swap_send.at[s, b], swap_recv.at[kind, lax.rem(at, 2), x],
                    (2 * column(p) + b, side, at // 2), final))

        def go():
            if direct(p):
                for d in range(1, DEPTH):
                    other = index[p, d]
                    near_copies[p, d].wait_recv()
                    keep[me] = keep[me] + unpack(near_in.at[other], 0, share)
            else:
                pltpu.make_async_copy(far_in.at[me], far_in.at[me], far_recv.at[me]).wait()
                keep[me] = keep[me] + unpack(far_in.at[me], 0, share)
            if copies:
                flipped = keep[me].T
                for b, copy in enumerate(copies):
                    pack(swap_out.at[s, b], [flipped[b * share:(b + 1) * share, :]])
                    copy.start()
            if not kind:
                show(row * lines + (column(p) - 2 * col) * wide, keep[me])

        when(final, go)

    def swapped(kind, l):
        for b in range(2):
            pltpu.make_async_copy(swap_in.at[kind, l, b], swap_in.at[kind, l, b], swap_recv.at[kind, l, b]).wait()
            joined[:, b * share:(b + 1) * share] = unpack(swap_in.at[kind, l, b], 0, share)

    def close(kind, l):
        if kind:
            swapped(1, l)
            show((1 - row) * lines + l * wide, joined[...] + keep[index[2 + l, 0]])
            return
        steps = lax.rem(z - (2 * col + l) + DEPTH, DEPTH)
        absent = steps > jnp.where(col == l, 2, 1)

        def go():
            swapped(0, l)
            show(row * lines + l * wide, joined[...])

        when(absent, go)

    def arrive(half):
        for chunk in range(2):
            row_copies[half, chunk].wait()

    for copy in col_copies:
        copy.wait_recv()
    plan = [(multiply, 0), (multiply, 1), (retain, 0), (retain, 1), (multiply, 2), (retain, 2),
            (take, 0, 0), (arrive, 0), (multiply, 3), (multiply, 4), (relay, 0, 0), (take, 0, 1), (take, 0, 2),
            (retain, 3), (retain, 4), (take, 1, 1), (relay, 0, 1), (relay, 0, 2), (finish, 0, 0),
            (relay, 1, 1), (take, 2, 3), (take, 2, 2), (finish, 0, 1), (finish, 0, 2), (arrive, 1),
            (multiply, 5), (multiply, 6), (multiply, 7), (multiply, 8), (multiply, 9),
            (finish, 1, 1), (relay, 2, 2), (retain, 5), (retain, 6), (retain, 7), (retain, 8), (retain, 9),
            (take, 2, 1), (take, 2, 0), (relay, 2, 0), (close, 0, 0), (close, 0, 1),
            (take, 3, 3), (finish, 2, 0), (take, 3, 2), (take, 3, 1), (take, 3, 0), (take, 1, 0),
            (close, 1, 0), (relay, 1, 0), (finish, 3, 0), (finish, 1, 0), (close, 1, 1)]
    for task, *which in plan:
        task(*which)
    for copy, condition in pending:
        when(condition, copy.wait_send)


def fused(coupling, factor_inv, block_mask):
    groups, order, width = coupling.shape
    depth, share = groups * order, width // DEPTH
    block, message, count = 2 * share, HEAD + share, len(keys_of())
    hbm = pl.BlockSpec(memory_space=pl.ANY)
    packets = [pltpu.VMEM((HEAD + share * len(es), block), LINK) for _, es in GROUPS]
    tile = pl.pallas_call(
        kernel,
        out_shape=jax.ShapeDtypeStruct((share * 2 * width // LANES, LANES), jnp.float32),
        in_specs=[hbm, hbm, pl.BlockSpec(memory_space=pltpu.SMEM)],
        out_specs=pl.BlockSpec(memory_space=pltpu.VMEM),
        scratch_shapes=[
            pltpu.VMEM((groups, order, width), jnp.bfloat16),
            pltpu.VMEM((groups, order, order), jnp.bfloat16),
            pltpu.VMEM((width, depth), jnp.bfloat16),
            pltpu.VMEM((2, width, depth), jnp.bfloat16),
            pltpu.VMEM((width, depth // 2), jnp.bfloat16),
            pltpu.VMEM((count, share, block), jnp.float32),
            pltpu.VMEM((2, share, block), jnp.float32),
            pltpu.VMEM((share, block), jnp.float32),
            pltpu.VMEM((count, message, block), LINK),
            pltpu.VMEM((count, message, block), LINK),
            pltpu.VMEM((count, message, block), LINK),
            pltpu.VMEM((len(SWAPS), 2, message, share), LINK),
            pltpu.VMEM((2, 2, 2, message, share), LINK),
            pltpu.SemaphoreType.DMA((groups, 2)),
            pltpu.SemaphoreType.DMA((groups,)),
            pltpu.SemaphoreType.DMA((groups,)),
            pltpu.SemaphoreType.DMA((2, 2)),
            pltpu.SemaphoreType.DMA((2, 2)),
            pltpu.SemaphoreType.DMA((len(GROUPS),)),
            pltpu.SemaphoreType.DMA((len(GROUPS),)),
            pltpu.SemaphoreType.DMA((count,)),
            pltpu.SemaphoreType.DMA((count,)),
            pltpu.SemaphoreType.DMA((count,)),
            pltpu.SemaphoreType.DMA((len(SWAPS), 2)),
            pltpu.SemaphoreType.DMA((2, 2, 2)),
            *packets, *packets,
        ],
        compiler_params=pltpu.CompilerParams(
            collective_id=0, has_side_effects=True, vmem_limit_bytes=52 * 1024 * 1024),
    )(coupling, factor_inv, block_mask)
    return tile.reshape(1, share, 2, 1, width)


def plain(coupling, factor_inv, block_mask):
    groups, order, width = coupling.shape
    spread = jnp.broadcast_to(
        block_mask[:, :, None, :, None], (groups, order // BLK, BLK, width // BLK, BLK)
    )
    masked = coupling * spread.reshape(groups, order, width).astype(jnp.bfloat16)
    solved = jnp.einsum(
        "snk,skw->snw", factor_inv, masked, preferred_element_type=jnp.float32
    ).astype(jnp.bfloat16)
    left = lax.all_gather(solved, "col", axis=2, tiled=True)
    share = left.shape[2] // lax.axis_size("scen")
    tile = lax.dot_general(
        left,
        lax.all_gather(solved, "row", axis=2, tiled=True),
        (((0, 1), (0, 1)), ((), ())),
        preferred_element_type=jnp.float32,
    )
    summed = lax.psum_scatter(tile, "scen", scatter_dimension=0, tiled=True)
    return summed.reshape(1, share, summed.shape[1] // width, 1, width)


def solution(mesh):
    n, n_row = mesh.shape["scen"], mesh.shape["row"]

    def shards(coupling, factor_inv, block_mask):
        groups, order, width = coupling.shape
        if n == 2 * DEPTH and n_row == 2 and (groups, order, width) == (3, 512, 768):
            return fused(coupling, factor_inv, block_mask)
        return plain(coupling, factor_inv, block_mask)

    in_specs = (
        P("scen", None, ("row", "col")),
        P("scen", None, None),
        P("scen", None, ("row", "col")),
    )
    out_specs = P("row", "scen", None, "col", None)
    return jax.shard_map(shards, mesh=mesh, in_specs=in_specs, out_specs=out_specs, check_vma=False)
```

time: 79.1 us -> 92 us (1.16)
  the two profiles are of different devices: /device:TPU:0 before, /device:TPU:11 now
where the time goes in v2:
time: 92 us; the launch traced here: 91.8 us
  Pallas kernels  90.1 us (98%)
  local copies, waits for them, and re-layouts  1.71 us (2%)
    pallas_call x1, Pallas kernels, fused(): pl.pallas_call(kernel, out_shape=jax.ShapeDtypeStruct((share * 2 * width...  90.1 us

profile of v2, /device:TPU:11, one launch (start us, length us, event | category | flops | bytes accessed | tf_op | source)
XLA Modules:
  0.0 91.8 jit_solution(14341438074432549733)
XLA Ops:
  0.0 0.0 copy-start
  0.0 0.7 copy-done
  0.7 90.1 %shard_map.37 = f32[2304,128]{1,0:T(8,128)S(1)} custom-call(bf16[3,512,768]{2,1,0:T(8,128)(2,1)} %coupling.1, bf16[3,512,512]{2,1,0:T(8,128)(2,1)} %factor.1, s32[3,4,6]{2,1,0:T(4,128)S(1)} %copy-done), custom_call_target="tpu_custom_call" | custom-call | tf_op jit(solution)/shard_map/pallas_call | solution.py:337
  90.8 1.0 %copy.6 = f32[1,192,2,1,768]{4,3,2,1,0:T(1,128)} copy(f32[1,192,2,1,768]{4,3,2,1,0:T(1,128)S(1)} %bitcast.1) | data formatting | bytes 2359296
Async XLA Ops:
  0.0 0.7 copy-start

commit v3 on v2

v3 whole, which is shorter than its diff:
```python
import functools

import jax
import jax.numpy as jnp
from jax import lax
from jax.experimental import pallas as pl
from jax.experimental.pallas import tpu as pltpu
from jax.sharding import PartitionSpec as P

BLK = 128
LANES = 128
HEAD = 16
LINK = jnp.int16
FINE = 64.0
TOP = 14.9
DEPTH = 4
MESH = pl.DeviceIdType.MESH
NT = (((1,), (1,)), ((), ()))
PIECES = (3, 2)
LATE = ((0, 256), (256, 256), (512, 128), (640, 128))
SWAPS = ((0, 1), (0, 2), (1, 1))
GROUPS = ((0, (0,)), (0, (1, 2)), (1, (1,)), (1, (0,)))
LATE_GROUPS = ((0, (3, 2)), (0, (1, 0)), (1, (3, 2)), (1, (1, 0)), (2, (3, 2)), (2, (1, 0)),
               (3, (3,)), (3, (2,)), (3, (1,)), (3, (0,)))
ORDER = (3, 2, 1, 0)


def power_of(values):
    most = jnp.max(jnp.abs(values[0]), axis=0, keepdims=True)
    for value in values[1:]:
        most = jnp.maximum(most, jnp.max(jnp.abs(value), axis=0, keepdims=True))
    return jnp.ceil(jnp.log2(jnp.maximum(most, 1e-30)) * FINE)


def pack(ref, values):
    power = power_of(values)
    scale = jnp.exp2(TOP - power / FINE)
    ref[0:HEAD, :] = jnp.broadcast_to(power, (HEAD, power.shape[1])).astype(jnp.int32).astype(LINK)
    start = HEAD
    for value in values:
        count = value.shape[0]
        ref[start:start + count, :] = jnp.round(value * scale).astype(jnp.int32).astype(LINK)
        start += count


def unpack(ref, start, count):
    power = ref[0:HEAD, :].astype(jnp.int32).astype(jnp.float32)[0:1, :]
    scaled = ref[HEAD + start:HEAD + start + count, :].astype(jnp.int32).astype(jnp.float32)
    return scaled * jnp.exp2(power / FINE - TOP)


def pack_square(ref, value):
    side = value.shape[0]
    power = power_of([value])
    scaled = jnp.round(value * jnp.exp2(TOP - power / FINE))
    heads = (power[:, :LANES], jnp.concatenate([power[:, LANES:]] * 2, axis=1))
    rest = jnp.concatenate([scaled[:side // 2, LANES:], scaled[side // 2:, LANES:]], axis=1)
    start = 0
    for head, body in zip(heads, (scaled[:, :LANES], rest)):
        ref[start:start + HEAD, :] = jnp.broadcast_to(head, (HEAD, LANES)).astype(jnp.int32).astype(LINK)
        ref[start + HEAD:start + HEAD + body.shape[0], :] = body.astype(jnp.int32).astype(LINK)
        start += HEAD + body.shape[0]


def unpack_square(ref, to, base, side):
    to[:, base:base + LANES] = unpack(ref, 0, side)
    rest = unpack(ref.at[HEAD + side:], 0, side // 2)
    more = side - LANES
    to[0:side // 2, base + LANES:base + side] = rest[:, :more]
    to[side // 2:, base + LANES:base + side] = rest[:, more:]


INDEX = {key: i for i, key in enumerate((p, e) for p, size in enumerate(PIECES) for e in range(size))}


def kernel(coupling, factor, mask, out, c_in, f_in, own, left, right, away, keep, joined,
           z_out, near_in, far_in, swap_out, swap_in,
           in_sem, col_send, col_recv, row_send, row_recv, x_send, x_recv, lx_send, lx_recv,
           z_send, near_recv, far_recv, swap_send, swap_recv, lz_send, lz_recv, *buffers):
    groups, order, width = coupling.shape
    share = width // DEPTH
    block = 2 * share
    lines = width // LANES
    sizes = (len(GROUPS), len(GROUPS), len(LATE_GROUPS), len(LATE_GROUPS), len(LATE), len(LATE), len(LATE))
    parts, start = [], 0
    for size in sizes:
        parts.append(buffers[start:start + size])
        start += size
    x_out, x_in, lx_out, lx_in, l_keep, lz_out, lz_in = parts
    scen, row, col = lax.axis_index("scen"), lax.axis_index("row"), lax.axis_index("col")
    z, x = scen // 2, lax.rem(scen, 2)
    near = z + 1 - 2 * lax.rem(z, 2)
    far = lax.rem(z + 2, DEPTH)
    apart = (z, near, far, DEPTH - 1 - z)
    across = (2 * z + 1 - x, row, col)
    opposite = (scen, 1 - row, col)
    sibling = (scen, row, 1 - col)

    loads = []
    for g in range(groups):
        pair = []
        for src, dst, k in ((coupling, c_in, 0), (factor, f_in, 1)):
            load = pltpu.make_async_copy(src.at[g], dst.at[g], in_sem.at[g, k])
            load.start()
            pair.append(load)
        loads.append(pair)

    barrier = pltpu.get_barrier_semaphore()
    peers = [across, opposite, sibling] + [(2 * level + x, row, col) for level in apart[1:]]
    for peer in peers:
        pl.semaphore_signal(barrier, inc=1, device_id=peer, device_id_type=MESH)

    pending = []

    def remote(src, dst, send_sem, recv_sem, device, condition=None):
        copy = pltpu.make_async_remote_copy(
            src_ref=src, dst_ref=dst, send_sem=send_sem, recv_sem=recv_sem,
            device_id=device, device_id_type=MESH)
        pending.append((copy, condition))
        if condition is None:
            copy.start()
        return copy

    col_copies, row_copies = [], {}

    def send_row(k, g, count):
        base, w = LATE[k]
        rows, lanes = pl.ds(base, w), pl.ds(g * order, count * order)
        row_copies[k, g] = remote(
            own.at[rows, lanes], right.at[rows, lanes], row_send.at[k, g], row_recv.at[k, g], opposite)

    for g in range(groups):
        for load in loads[g]:
            load.wait()
        rows = []
        for i in range(order // BLK):
            rows.append(jnp.concatenate([
                c_in[g, i * BLK:(i + 1) * BLK, j * BLK:(j + 1) * BLK]
                * mask[g, i, j].astype(jnp.float32).astype(jnp.bfloat16)
                for j in range(width // BLK)], axis=1))
        masked = jnp.concatenate(rows, axis=0)
        solved = jnp.dot(f_in[g], masked, preferred_element_type=jnp.float32)
        turned = solved.T.astype(jnp.bfloat16)
        lanes = slice(g * order, (g + 1) * order)
        own[:, lanes] = turned
        if g == 0:
            pl.semaphore_wait(barrier, len(peers))
        send_row(0, g, 1)
        for a in range(2):
            for b in range(2):
                at = pl.multiple_of(col * block + a * share, share)
                left[b, pl.ds(at, share), lanes] = turned[(2 * a + b) * share:(2 * a + b + 1) * share]
        mine = left.at[:, pl.ds(pl.multiple_of(col * block, block), block), pl.ds(g * order, order)]
        col_copies.append(remote(mine, mine, col_send.at[g], col_recv.at[g], sibling))
    for k in range(1, len(LATE)):
        send_row(k, 0, groups)

    def column(p):
        return 3 * col if p == 0 else 1 + col

    def level(p, e):
        return lax.rem(column(p) + e, DEPTH)

    def slab(at):
        return pl.ds(pl.multiple_of(at * share, share), share)

    def product(b, p, e):
        rhs = own[pl.ds(pl.multiple_of((col if p == 0 else 1 - col) * block, block), block), :]
        return lax.dot_general(left[b, slab(level(p, e)), :], rhs, NT, preferred_element_type=jnp.float32)

    def late_product(b, p, d):
        base, w = LATE[p]
        return lax.dot_general(left[b, slab(apart[d]), :], right[base:base + w, :], NT,
                               preferred_element_type=jnp.float32)

    x_copies, lx_copies, lz_copies = {}, {}, {}
    place_of = {(p, e): (k, i) for k, (p, es) in enumerate(GROUPS) for i, e in enumerate(es)}
    late_place = {(p, d): (k, i) for k, (p, ds) in enumerate(LATE_GROUPS) for i, d in enumerate(ds)}

    def multiply(k):
        p, es = GROUPS[k]
        for i, e in enumerate(es):
            away[i] = product(1 - x, p, e)
        pack(x_out[k], [away[i] for i in range(len(es))])
        x_copies[k] = remote(x_out[k], x_in[k], x_send.at[k], x_recv.at[k], across)

    def retain(k):
        p, es = GROUPS[k]
        for e in es:
            keep[INDEX[p, e]] = product(x, p, e)

    def take(p, e):
        k, i = place_of[p, e]
        if i == 0:
            x_copies[k].wait_recv()
        me, at = INDEX[p, e], level(p, e)
        differ = lax.rem(z + at, 2) == 1
        copy = remote(z_out.at[me], near_in.at[me], z_send.at[me], near_recv.at[me], (2 * near + x, row, col), differ)
        keep[me] = keep[me] + unpack(x_in[k], i * share, share)

        @pl.when(differ)
        def _():
            pack(z_out.at[me], [keep[me]])
            copy.start()

    def relay(p, e):
        me, at = INDEX[p, e], level(p, e)
        passed = far == at
        copy = remote(z_out.at[me], far_in.at[me], z_send.at[me], far_recv.at[me], (2 * far + x, row, col), passed)

        @pl.when(lax.rem(z + at, 2) == 0)
        def _():
            pltpu.make_async_copy(near_in.at[me], near_in.at[me], near_recv.at[me]).wait()
            keep[me] = keep[me] + unpack(near_in.at[me], 0, share)

        @pl.when(passed)
        def _():
            pack(z_out.at[me], [keep[me]])
            copy.start()

    def show(place, value):
        for c in range(value.shape[1] // LANES):
            out[pl.ds(place + c, share, stride=2 * lines), :] = value[:, c * LANES:(c + 1) * LANES]

    def finish(p, e):
        me, at = INDEX[p, e], level(p, e)
        final = z == at
        copies = []
        if (p, e) in SWAPS:
            s = SWAPS.index((p, e))
            for b in range(2):
                copies.append(remote(
                    swap_out.at[s, b], swap_in.at[lax.rem(at, 2), x],
                    swap_send.at[s, b], swap_recv.at[lax.rem(at, 2), x],
                    (2 * column(p) + b, row, at // 2), final))

        @pl.when(final)
        def _():
            pltpu.make_async_copy(far_in.at[me], far_in.at[me], far_recv.at[me]).wait()
            keep[me] = keep[me] + unpack(far_in.at[me], 0, share)
            if copies:
                flipped = keep[me].T
                for b, copy in enumerate(copies):
                    pack_square(swap_out.at[s, b], flipped[b * share:(b + 1) * share, :])
                    copy.start()
            show(row * lines + (column(p) - 2 * col) * (block // LANES), keep[me])

    def close(l):
        steps = lax.rem(z - (2 * col + l) + DEPTH, DEPTH)

        @pl.when(steps > jnp.where(col == l, 2, 1))
        def _():
            for b in range(2):
                pltpu.make_async_copy(swap_in.at[l, b], swap_in.at[l, b], swap_recv.at[l, b]).wait()
                unpack_square(swap_in.at[l, b], joined, b * share, share)
            show(row * lines + l * (block // LANES), joined[...])

    def gather():
        for copy in col_copies:
            copy.wait_recv()

    def arrive(p):
        for g in range(groups if p == 0 else 1):
            row_copies[p, g].wait_recv()

    def late_multiply(k):
        p, ds = LATE_GROUPS[k]
        w = LATE[p][1]
        for i, d in enumerate(ds):
            away[i, :, 0:w] = late_product(1 - x, p, d)
        pack(lx_out[k], [away[i, :, 0:w] for i in range(len(ds))])
        lx_copies[k] = remote(lx_out[k], lx_in[k], lx_send.at[k], lx_recv.at[k], across)

    def late_retain(p):
        for d in ORDER:
            l_keep[p][d] = late_product(x, p, d)

    def late_take(p, d):
        k, i = late_place[p, d]
        if i == 0:
            lx_copies[k].wait_recv()
        value = l_keep[p][d] + unpack(lx_in[k], i * share, share)
        if d == 0:
            l_keep[p][0] = value
            return
        pack(lz_out[p].at[d], [value])
        lz_copies[p, d] = remote(
            lz_out[p].at[d], lz_in[p].at[d], lz_send.at[p, d], lz_recv.at[p, d], (2 * apart[d] + x, row, col))

    def late_finish(p):
        value = l_keep[p][0]
        for d in ORDER[:-1]:
            lz_copies[p, d].wait_recv()
            value += unpack(lz_in[p].at[d], 0, share)
        show((1 - row) * lines + LATE[p][0] // LANES, value)

    plan = [(multiply, 0), (gather,), (multiply, 1), (multiply, 2), (multiply, 3),
            (retain, 0), (retain, 1), (retain, 2), (retain, 3),
            (take, 0, 0), (take, 0, 1), (take, 0, 2), (relay, 0, 0), (arrive, 0),
            (late_multiply, 0), (late_multiply, 1), (late_retain, 0),
            (take, 1, 1), (relay, 0, 1), (relay, 0, 2), (finish, 0, 0), (finish, 0, 1), (finish, 0, 2),
            (take, 1, 0), (relay, 1, 1), (relay, 1, 0), (finish, 1, 1),
            (late_take, 0, 3), (late_take, 0, 2), (finish, 1, 0), (late_take, 0, 1), (late_take, 0, 0),
            (close, 0), (close, 1), (arrive, 1), (late_multiply, 2), (late_multiply, 3), (late_retain, 1), (late_finish, 0),
            (late_take, 1, 3), (late_take, 1, 2), (arrive, 2), (late_multiply, 4), (late_multiply, 5), (late_retain, 2),
            (late_take, 1, 1), (late_take, 1, 0), (late_take, 2, 3), (late_take, 2, 2), (arrive, 3),
            (late_multiply, 6), (late_multiply, 7), (late_multiply, 8), (late_multiply, 9),
            (late_take, 2, 1), (late_take, 2, 0), (late_retain, 3), (late_finish, 1),
            (late_take, 3, 3), (late_take, 3, 2), (late_finish, 2), (late_take, 3, 1), (late_take, 3, 0), (late_finish, 3)]
    for task, *which in plan:
        task(*which)
    for copy, condition in pending:
        if condition is None:
            copy.wait_send()
        else:
            pl.when(condition)(copy.wait_send)


def fused(coupling, factor_inv, block_mask):
    groups, order, width = coupling.shape
    depth, share = groups * order, width // DEPTH
    block, message, count = 2 * share, HEAD + share, len(INDEX)
    square = 2 * HEAD + share + share // 2
    hbm = pl.BlockSpec(memory_space=pl.ANY)
    packets = [pltpu.VMEM((HEAD + share * len(es), block), LINK) for _, es in GROUPS]
    late_packets = [pltpu.VMEM((HEAD + share * len(ds), LATE[p][1]), LINK) for p, ds in LATE_GROUPS]
    sums = [pltpu.VMEM((DEPTH, share, w), jnp.float32) for _, w in LATE]
    messages = [pltpu.VMEM((DEPTH, message, w), LINK) for _, w in LATE]
    dma = pltpu.SemaphoreType.DMA
    tile = pl.pallas_call(
        kernel,
        out_shape=jax.ShapeDtypeStruct((share * 2 * width // LANES, LANES), jnp.float32),
        in_specs=[hbm, hbm, pl.BlockSpec(memory_space=pltpu.SMEM)],
        out_specs=pl.BlockSpec(memory_space=pltpu.VMEM),
        scratch_shapes=[
            pltpu.VMEM((groups, order, width), jnp.bfloat16),
            pltpu.VMEM((groups, order, order), jnp.bfloat16),
            pltpu.VMEM((width, depth), jnp.bfloat16),
            pltpu.VMEM((2, width, depth), jnp.bfloat16),
            pltpu.VMEM((width, depth), jnp.bfloat16),
            pltpu.VMEM((2, share, block), jnp.float32),
            pltpu.VMEM((count, share, block), jnp.float32),
            pltpu.VMEM((share, block), jnp.float32),
            pltpu.VMEM((count, message, block), LINK),
            pltpu.VMEM((count, message, block), LINK),
            pltpu.VMEM((count, message, block), LINK),
            pltpu.VMEM((len(SWAPS), 2, square, LANES), LINK),
            pltpu.VMEM((2, 2, square, LANES), LINK),
            dma((groups, 2)), dma((groups,)), dma((groups,)),
            dma((len(LATE), groups)), dma((len(LATE), groups)),
            dma((len(GROUPS),)), dma((len(GROUPS),)),
            dma((len(LATE_GROUPS),)), dma((len(LATE_GROUPS),)),
            dma((count,)), dma((count,)), dma((count,)),
            dma((len(SWAPS), 2)), dma((2, 2)),
            dma((len(LATE), DEPTH)), dma((len(LATE), DEPTH)),
            *packets, *packets, *late_packets, *late_packets, *sums, *messages, *messages,
        ],
        compiler_params=pltpu.CompilerParams(
            collective_id=0, has_side_effects=True, vmem_limit_bytes=52 * 1024 * 1024),
    )(coupling, factor_inv, block_mask)
    return tile.reshape(1, share, 2, 1, width)


def plain(coupling, factor_inv, block_mask):
    groups, order, width = coupling.shape
    spread = jnp.broadcast_to(
        block_mask[:, :, None, :, None], (groups, order // BLK, BLK, width // BLK, BLK)
    )
    masked = coupling * spread.reshape(groups, order, width).astype(jnp.bfloat16)
    solved = jnp.einsum(
        "snk,skw->snw", factor_inv, masked, preferred_element_type=jnp.float32
    ).astype(jnp.bfloat16)
    left = lax.all_gather(solved, "col", axis=2, tiled=True)
    share = left.shape[2] // lax.axis_size("scen")
    tile = lax.dot_general(
        left,
        lax.all_gather(solved, "row", axis=2, tiled=True),
        (((0, 1), (0, 1)), ((), ())),
        preferred_element_type=jnp.float32,
    )
    summed = lax.psum_scatter(tile, "scen", scatter_dimension=0, tiled=True)
    return summed.reshape(1, share, summed.shape[1] // width, 1, width)


def solution(mesh):
    n, n_row = mesh.shape["scen"], mesh.shape["row"]

    def shards(coupling, factor_inv, block_mask):
        groups, order, width = coupling.shape
        if n == 2 * DEPTH and n_row == 2 and (groups, order, width) == (3, 512, 768):
            return fused(coupling, factor_inv, block_mask)
        return plain(coupling, factor_inv, block_mask)

    in_specs = (
        P("scen", None, ("row", "col")),
        P("scen", None, None),
        P("scen", None, ("row", "col")),
    )
    out_specs = P("row", "scen", None, "col", None)
    return jax.shard_map(shards, mesh=mesh, in_specs=in_specs, out_specs=out_specs, check_vma=False)
```

time: 92 us -> 75.2 us (0.82)
  the two profiles are of different devices: /device:TPU:11 before, /device:TPU:1 now
where the time goes in v3:
time: 75.2 us; the launch traced here: 75 us
  Pallas kernels  73.3 us (97%)
  local copies, waits for them, and re-layouts  1.71 us (2%)
    pallas_call x1, Pallas kernels, fused(): pl.pallas_call(kernel, out_shape=jax.ShapeDtypeStruct((share * 2 * width...  73.3 us
    unnamed x3, local copies, waits for them, and re-layouts  1.71 us

profile of v3, /device:TPU:1, one launch (start us, length us, event | category | flops | bytes accessed | tf_op | source)
XLA Modules:
  0.0 75.0 jit_solution(15576461291366693063)
XLA Ops:
  0.0 0.0 copy-start
  0.0 0.7 copy-done
  0.7 73.3 %shard_map.37 = f32[2304,128]{1,0:T(8,128)S(1)} custom-call(bf16[3,512,768]{2,1,0:T(8,128)(2,1)} %coupling.1, bf16[3,512,512]{2,1,0:T(8,128)(2,1)} %factor.1, s32[3,4,6]{2,1,0:T(4,128)S(1)} %copy-done), custom_call_target="tpu_custom_call" | custom-call | tf_op jit(solution)/shard_map/pallas_call | solution.py:330
  74.0 1.0 %copy.6 = f32[1,192,2,1,768]{4,3,2,1,0:T(1,128)} copy(f32[1,192,2,1,768]{4,3,2,1,0:T(1,128)S(1)} %bitcast.1) | data formatting | bytes 2359296
Async XLA Ops:
  0.0 0.7 copy-start

commit v4 on v3

--- a/solution.py
+++ b/solution.py
@@ -294,19 +294,17 @@
             value += unpack(lz_in[p].at[d], 0, share)
         show((1 - row) * lines + LATE[p][0] // LANES, value)
 
-    plan = [(multiply, 0), (gather,), (multiply, 1), (multiply, 2), (multiply, 3),
-            (retain, 0), (retain, 1), (retain, 2), (retain, 3),
-            (take, 0, 0), (take, 0, 1), (take, 0, 2), (relay, 0, 0), (arrive, 0),
-            (late_multiply, 0), (late_multiply, 1), (late_retain, 0),
-            (take, 1, 1), (relay, 0, 1), (relay, 0, 2), (finish, 0, 0), (finish, 0, 1), (finish, 0, 2),
-            (take, 1, 0), (relay, 1, 1), (relay, 1, 0), (finish, 1, 1),
-            (late_take, 0, 3), (late_take, 0, 2), (finish, 1, 0), (late_take, 0, 1), (late_take, 0, 0),
-            (close, 0), (close, 1), (arrive, 1), (late_multiply, 2), (late_multiply, 3), (late_retain, 1), (late_finish, 0),
-            (late_take, 1, 3), (late_take, 1, 2), (arrive, 2), (late_multiply, 4), (late_multiply, 5), (late_retain, 2),
-            (late_take, 1, 1), (late_take, 1, 0), (late_take, 2, 3), (late_take, 2, 2), (arrive, 3),
-            (late_multiply, 6), (late_multiply, 7), (late_multiply, 8), (late_multiply, 9),
-            (late_take, 2, 1), (late_take, 2, 0), (late_retain, 3), (late_finish, 1),
-            (late_take, 3, 3), (late_take, 3, 2), (late_finish, 2), (late_take, 3, 1), (late_take, 3, 0), (late_finish, 3)]
+    plan = [(multiply, 0), (gather,), (multiply, 1), (multiply, 2), (multiply, 3), (retain, 0), (retain, 1),
+            (retain, 2), (retain, 3), (take, 0, 0), (take, 0, 1), (take, 0, 2), (relay, 0, 0), (arrive, 0),
+            (late_multiply, 0), (late_multiply, 1), (late_retain, 0), (take, 1, 1), (relay, 0, 1), (relay, 0, 2),
+            (finish, 0, 0), (finish, 0, 1), (finish, 0, 2), (late_take, 0, 3), (late_take, 0, 2), (take, 1, 0),
+            (relay, 1, 1), (relay, 1, 0), (arrive, 1), (late_multiply, 2), (late_multiply, 3), (late_take, 0, 1),
+            (late_take, 0, 0), (late_retain, 1), (late_finish, 0), (finish, 1, 1), (finish, 1, 0), (late_take, 1, 3),
+            (arrive, 2), (late_multiply, 4), (late_multiply, 5), (late_take, 1, 2), (late_retain, 2),
+            (late_take, 1, 1), (late_take, 1, 0), (late_take, 2, 3), (late_take, 2, 2), (close, 0), (close, 1),
+            (arrive, 3), (late_multiply, 6), (late_multiply, 7), (late_multiply, 8), (late_multiply, 9),
+            (late_take, 2, 1), (late_take, 2, 0), (late_retain, 3), (late_take, 3, 3), (late_take, 3, 2),
+            (late_finish, 1), (late_finish, 2), (late_take, 3, 1), (late_take, 3, 0), (late_finish, 3)]
     for task, *which in plan:
         task(*which)
     for copy, condition in pending:

time: 75.2 us -> 73.1 us (0.972)
  the two profiles are of different devices: /device:TPU:1 before, /device:TPU:0 now
where the time goes in v4:
time: 73.1 us; the launch traced here: 72.9 us
  Pallas kernels  71.2 us (97%)
  local copies, waits for them, and re-layouts  1.71 us (2%)
    pallas_call x1, Pallas kernels, fused(): pl.pallas_call(kernel, out_shape=jax.ShapeDtypeStruct((share * 2 * width...  71.2 us
    unnamed x3, local copies, waits for them, and re-layouts  1.71 us

profile of v4, /device:TPU:0, one launch (start us, length us, event | category | flops | bytes accessed | tf_op | source)
XLA Modules:
  0.0 72.9 jit_solution(6554395782417315699)
XLA Ops:
  0.0 0.0 copy-start
  0.0 0.7 copy-done
  0.7 71.2 %shard_map.37 = f32[2304,128]{1,0:T(8,128)S(1)} custom-call(bf16[3,512,768]{2,1,0:T(8,128)(2,1)} %coupling.1, bf16[3,512,512]{2,1,0:T(8,128)(2,1)} %factor.1, s32[3,4,6]{2,1,0:T(4,128)S(1)} %copy-done), custom_call_target="tpu_custom_call" | custom-call | tf_op jit(solution)/shard_map/pallas_call | solution.py:328
  71.9 1.0 %copy.6 = f32[1,192,2,1,768]{4,3,2,1,0:T(1,128)} copy(f32[1,192,2,1,768]{4,3,2,1,0:T(1,128)S(1)} %bitcast.1) | data formatting | bytes 2359296
Async XLA Ops:
  0.0 0.7 copy-start

commit v5 on v4

--- a/solution.py
+++ b/solution.py
@@ -139,7 +139,10 @@
                 * mask[g, i, j].astype(jnp.float32).astype(jnp.bfloat16)
                 for j in range(width // BLK)], axis=1))
         masked = jnp.concatenate(rows, axis=0)
-        solved = jnp.dot(f_in[g], masked, preferred_element_type=jnp.float32)
+        top = order // 2
+        solved = jnp.concatenate([
+            jnp.dot(f_in[g, :top, :top], masked[:top], preferred_element_type=jnp.float32),
+            jnp.dot(f_in[g, top:], masked, preferred_element_type=jnp.float32)], axis=0)
         turned = solved.T.astype(jnp.bfloat16)
         lanes = slice(g * order, (g + 1) * order)
         own[:, lanes] = turned

time: 73.1 us -> 72.8 us (level)
  no operation moved by 1% of the time
where the time goes in v5:
time: 72.8 us; the launch traced here: 72.4 us
  Pallas kernels  70.7 us (97%)
  local copies, waits for them, and re-layouts  1.71 us (2%)
    pallas_call x1, Pallas kernels, fused(): pl.pallas_call(kernel, out_shape=jax.ShapeDtypeStruct((share * 2 * width...  70.7 us
    unnamed x3, local copies, waits for them, and re-layouts  1.71 us

profile of v5, /device:TPU:0, one launch (start us, length us, event | category | flops | bytes accessed | tf_op | source)
XLA Modules:
  0.0 72.4 jit_solution(13582453961863402445)
XLA Ops:
  0.0 0.0 copy-start
  0.0 0.7 copy-done
  0.7 70.7 %shard_map.37 = f32[2304,128]{1,0:T(8,128)S(1)} custom-call(bf16[3,512,768]{2,1,0:T(8,128)(2,1)} %coupling.1, bf16[3,512,512]{2,1,0:T(8,128)(2,1)} %factor.1, s32[3,4,6]{2,1,0:T(4,128)S(1)} %copy-done), custom_call_target="tpu_custom_call" | custom-call | tf_op jit(solution)/shard_map/pallas_call | solution.py:331
  71.4 1.0 %copy.6 = f32[1,192,2,1,768]{4,3,2,1,0:T(1,128)} copy(f32[1,192,2,1,768]{4,3,2,1,0:T(1,128)S(1)} %bitcast.1) | data formatting | bytes 2359296
Async XLA Ops:
  0.0 0.7 copy-start

commit v6 on v4

--- a/solution.py
+++ b/solution.py
@@ -139,7 +139,9 @@
                 * mask[g, i, j].astype(jnp.float32).astype(jnp.bfloat16)
                 for j in range(width // BLK)], axis=1))
         masked = jnp.concatenate(rows, axis=0)
-        solved = jnp.dot(f_in[g], masked, preferred_element_type=jnp.float32)
+        solved = jnp.concatenate([
+            jnp.dot(f_in[g, end - BLK:end, :end], masked[:end], preferred_element_type=jnp.float32)
+            for end in range(BLK, order + 1, BLK)], axis=0)
         turned = solved.T.astype(jnp.bfloat16)
         lanes = slice(g * order, (g + 1) * order)
         own[:, lanes] = turned

time: 73.1 us -> 72.7 us (level)
  no operation moved by 1% of the time
where the time goes in v6:
time: 72.7 us; the launch traced here: 72.4 us
  Pallas kernels  70.7 us (97%)
  local copies, waits for them, and re-layouts  1.71 us (2%)
    pallas_call x1, Pallas kernels, fused(): pl.pallas_call(kernel, out_shape=jax.ShapeDtypeStruct((share * 2 * width...  70.7 us
    unnamed x3, local copies, waits for them, and re-layouts  1.71 us

profile of v6, /device:TPU:0, one launch (start us, length us, event | category | flops | bytes accessed | tf_op | source)
XLA Modules:
  0.0 72.4 jit_solution(8524566407375443512)
XLA Ops:
  0.0 0.0 copy-start
  0.0 0.7 copy-done
  0.7 70.7 %shard_map.37 = f32[2304,128]{1,0:T(8,128)S(1)} custom-call(bf16[3,512,768]{2,1,0:T(8,128)(2,1)} %coupling.1, bf16[3,512,512]{2,1,0:T(8,128)(2,1)} %factor.1, s32[3,4,6]{2,1,0:T(4,128)S(1)} %copy-done), custom_call_target="tpu_custom_call" | custom-call | tf_op jit(solution)/shard_map/pallas_call | solution.py:330
  71.4 1.0 %copy.6 = f32[1,192,2,1,768]{4,3,2,1,0:T(1,128)} copy(f32[1,192,2,1,768]{4,3,2,1,0:T(1,128)S(1)} %bitcast.1) | data formatting | bytes 2359296
Async XLA Ops:
  0.0 0.7 copy-start
